TPU v7x, 32 devices: a whole 2x2x4 slice. The times are simulated.
32 devices in a mesh: dp: 4 (over z), mp: 8 (over y, x, core).
Axes of the slice: x: 2, y: 2, z: 4, core: 2. Of those that a mesh axis runs over, the one named last changes fastest.
Arguments:
- gradients: bfloat16 [4, 2, 768, 2048], P('dp', None, None, 'mp'), may hold values from -4 to 4
- weights: bfloat16 [2, 768, 2048], P(None, None, 'mp'), may hold values from -4 to 4
- projection: float32 [2, 768, 256], replicated, may hold values from -0.21875 to 0.21875
- moment_first: float32 [2, 256, 2048], P(None, 'dp', 'mp'), may hold values from -6 to 6
- moment_second: float32 [2, 256, 2048], P(None, 'dp', 'mp'), may hold values from 0.25 to 4
Outputs:
- new_weights: bfloat16 [2, 768, 2048], P(None, None, 'mp')
- new_first: float32 [2, 256, 2048], P(None, 'dp', 'mp')
- new_second: float32 [2, 256, 2048], P(None, 'dp', 'mp')
- new_bases: float32 [2, 768, 256], replicated
All inputs are finite; a program needn't handle non-finite values.
Results may differ from a plain program's by a relative error of at most 0.0004.
Values may be sent and summed in bfloat16 or wider, within the bound.
A program may use at most 64 MiB of HBM per device.

v0:
```python
import jax
import jax.numpy as jnp
from jax import lax
from jax.sharding import PartitionSpec as P

NS_ITERS = 4
beta_first = 0.5
beta_second = 0.5
adam_eps = 1e-06
learn_rate = 0.1


def newton_schulz(subspace):
    highest = lax.Precision.HIGHEST
    factor = 1.0 / (jnp.sqrt(jnp.sum(subspace * subspace, axis=(1, 2), keepdims=True)) + 1e-06)
    current = subspace * factor
    for sweep in range(NS_ITERS):
        gram = jnp.einsum("ldr,lds->lrs", current, current, precision=highest)
        current = 1.5 * current - 0.5 * jnp.einsum("ldr,lrs->lds", current, gram, precision=highest)
    return current


def back_project(bases_rows, direction_own):
    highest = lax.Precision.HIGHEST
    return jnp.einsum(
        "ldr,lrf->ldf",
        bases_rows,
        lax.all_gather(direction_own, "dp", axis=1, tiled=True),
        precision=highest,
    )


def shards(gradients, weights, projection, moment_first, moment_second):
    highest = lax.Precision.HIGHEST
    local_grad = gradients[0].astype(jnp.float32)
    totals = lax.psum(local_grad, "dp")
    lowrank = jnp.einsum("ldr,ldf->lrf", projection, totals, precision=highest)
    partial_sub = jnp.einsum("ldf,lrf->ldr", totals, lowrank, precision=highest)
    subspace = lax.psum(partial_sub, "mp")
    rank_rows = moment_first.shape[1]
    rank_start = lax.axis_index("dp") * rank_rows
    low_own = lax.dynamic_slice_in_dim(lowrank, rank_start, rank_rows, 1)
    new_first = beta_first * moment_first + (1.0 - beta_first) * low_own
    new_second = beta_second * moment_second + (1.0 - beta_second) * low_own * low_own
    direction_own = new_first / (jnp.sqrt(new_second) + adam_eps)
    width_rows = weights.shape[1] // lax.axis_size("dp")
    row_start = lax.axis_index("dp") * width_rows
    bases_rows = lax.dynamic_slice_in_dim(projection, row_start, width_rows, 1)
    weight_rows = lax.dynamic_slice_in_dim(weights, row_start, width_rows, 1)
    delta_rows = back_project(bases_rows, direction_own)
    updated = (weight_rows.astype(jnp.float32) - learn_rate * delta_rows).astype(jnp.bfloat16)
    new_weights = lax.all_gather(updated, "dp", axis=1, tiled=True)
    new_bases = newton_schulz(subspace)
    return (new_weights, new_first, new_second, new_bases)


def solution(mesh):
    placed = (
        P("dp", None, None, "mp"),
        P(None, None, "mp"),
        P(),
        P(None, "dp", "mp"),
        P(None, "dp", "mp"),
    )
    return jax.shard_map(
        shards,
        mesh=mesh,
        in_specs=placed,
        out_specs=(P(None, None, "mp"), P(None, "dp", "mp"), P(None, "dp", "mp"), P()),
        check_vma=False,
    )
```

profile of v0, /device:TPU:0, one launch (start us, length us, event | category | flops | bytes accessed | tf_op | source)
XLA Modules:
  0.0 174.0 jit_solution(6145538785186923639)
XLA Ops:
  7.2 0.0 copy-start
  7.2 0.0 all-reduce.3.cloned.1.call-start
  7.2 2.5 %bitcast_convert_fusion = f32[2,768,256]{2,1,0:T(8,128)} fusion(bf16[1,2,768,256]{3,2,1,0:T(8,128)(2,1)} %param.5), kind=kLoop, calls=%fused_computation.12 | loop fusion | flops 393216 | bytes 2359296 | tf_op jit(solution)/shard_map/convert_element_type | solution.py:35
  9.7 0.0 all-reduce.3.cloned.1.call-update
  9.8 0.0 all-reduce.5.cloned.1.call-start
  9.8 72.8 %all-reduce.3.cloned.1.call-done = f32[2,768,256]{2,1,0:T(8,128)} async-done(((f32[2,768,256]{2,1,0:T(8,128)}), f32[2,768,256]{2,1,0:T(8,128)}) %all-reduce.3.cloned.1.call-update) | async-done | bytes 1572880 | tf_op jit(solution)/shard_map/psum | solution.py:36
  82.7 0.0 copy-done
  82.7 0.0 copy-start.2
  82.7 4.2 %fusion.11 = f32[2,256,256]{2,1,0:T(8,128)S(1)} fusion(f32[2,768,256]{2,1,0:T(8,128)S(1)} %copy-done, f32[2,768,256]{2,1,0:T(8,128)} %all-reduce.3.cloned.1.call-done), kind=kOutput, calls=%fused_computation.22 | convolution fusion | flops 1207959552 | bytes 3670016 | tf_op jit(solution)/shard_map/ldr,ldf->lrf/dot_general | solution.py:37
  86.9 0.0 copy-done.2
  86.9 2.6 %convolution_bitcast_fusion = f32[2,768,256]{1,2,0:T(8,128)} fusion(f32[2,256,256]{2,1,0:T(8,128)S(1)} %fusion.11, f32[2,768,256]{2,1,0:T(8,128)S(1)} %copy-done.2), kind=kOutput, calls=%fused_computation.5 | convolution fusion | flops 1207959552 | bytes 3670016 | tf_op jit(solution)/shard_map/ldf,lrf->ldr/dot_general | solution.py:38
  89.5 0.0 copy-start.3
  89.5 0.0 copy-start.4
  89.5 0.0 all-reduce.5.cloned.1.call-update
  89.5 0.9 copy-done.3
  90.4 0.1 copy-done.4
  90.5 0.8 add_divide_fusion
  91.2 15.7 %all_gather.6 = f32[2,256,256]{2,1,0:T(8,128)S(1)} all-gather(f32[2,64,256]{2,1,0:T(8,128)S(1)} %get-tuple-element.8), channel_id=1, replica_groups=mesh['dp'=4,'mp'=8] {'dp'}, dimensions={1}, use_global_device_ids=true | all-gather | bytes 655360 | tf_op jit(solution)/shard_map/all_gather | solution.py:28
  106.9 1.5 fusion.4
  108.4 18.3 %all_gather.7 = bf16[2,768,256]{2,1,0:T(8,128)(2,1)} all-gather(bf16[2,192,256]{2,1,0:T(8,128)(2,1)S(1)} %fusion.4), channel_id=1, replica_groups=mesh['dp'=4,'mp'=8] {'dp'}, dimensions={1}, use_global_device_ids=true | all-gather | bytes 983040 | tf_op jit(solution)/shard_map/all_gather | solution.py:52
  126.7 20.9 %all-reduce.5.cloned.1.call-done = f32[2,768,256]{1,2,0:T(8,128)} async-done(((f32[2,768,256]{1,2,0:T(8,128)}), f32[2,768,256]{1,2,0:T(8,128)}) %all-reduce.5.cloned.1.call-update) | async-done | bytes 1572880 | tf_op jit(solution)/shard_map/psum | solution.py:39
  147.6 0.0 copy-start.1
  147.6 1.8 %multiply_reduce_fusion = f32[2]{0:T(128)S(1)} fusion(f32[2,768,256]{1,2,0:T(8,128)} %all-reduce.5.cloned.1.call-done), kind=kLoop, calls=%fused_computation.4 | loop fusion | flops 786430 | bytes 1572872 | tf_op jit(solution)/shard_map/reduce_sum | solution.py:15
  149.4 0.0 copy-done.1
  149.5 1.8 %fusion = f32[2,256,256]{2,1,0:T(8,128)S(1)} fusion(f32[2,768,256]{1,2,0:T(8,128)S(1)} %copy-done.1, f32[2]{0:T(128)S(1)} %add_divide_fusion.1), kind=kOutput, calls=%fused_computation.6 | convolution fusion | flops 1208352768 | bytes 2097160 | tf_op jit(solution)/shard_map/ldr,lds->lrs/dot_general | solution.py:18
  151.2 2.0 %multiply_subtract_fusion.3 = f32[2,768,256]{1,2,0:T(8,128)S(1)} fusion(f32[2,256,256]{2,1,0:T(8,128)S(1)} %fusion, f32[2,768,256]{1,2,0:T(8,128)S(1)} %copy-done.1, f32[2]{0:T(128)S(1)} %add_divide_fusion.1), kind=kOutput, calls=%fused_computation.3 | convolution fusion | flops 1209925632 | bytes 3670024 | tf_op jit(solution)/shard_map/ldr,lrs->lds/dot_general | solution.py:19
  153.2 1.6 fusion.12
  154.9 1.8 %multiply_subtract_fusion.2 = f32[2,768,256]{1,2,0:T(8,128)S(1)} fusion(f32[2,768,256]{1,2,0:T(8,128)S(1)} %multiply_subtract_fusion.3, f32[2,256,256]{2,1,0:T(8,128)S(1)} %fusion.12), kind=kOutput, calls=%fused_computation.2 | convolution fusion | flops 1209139200 | bytes 3670016 | tf_op jit(solution)/shard_map/ldr,lrs->lds/dot_general | solution.py:19
  156.6 1.6 fusion.13
  158.3 1.8 %multiply_subtract_fusion.1 = f32[2,768,256]{1,2,0:T(8,128)S(1)} fusion(f32[2,768,256]{1,2,0:T(8,128)S(1)} %multiply_subtract_fusion.2, f32[2,256,256]{2,1,0:T(8,128)S(1)} %fusion.13), kind=kOutput, calls=%fused_computation.1 | convolution fusion | flops 1209139200 | bytes 3670016 | tf_op jit(solution)/shard_map/ldr,lrs->lds/dot_general | solution.py:19
  160.1 1.6 fusion.14
  161.7 1.8 %multiply_subtract_fusion = f32[2,768,256]{1,2,0:T(8,128)S(1)} fusion(f32[2,768,256]{1,2,0:T(8,128)S(1)} %multiply_subtract_fusion.1, f32[2,256,256]{2,1,0:T(8,128)S(1)} %fusion.14), kind=kOutput, calls=%fused_computation | convolution fusion | flops 1209139200 | bytes 3670016 | tf_op jit(solution)/shard_map/ldr,lrs->lds/dot_general | solution.py:19
  163.5 1.6 copy.18
  165.1 2.1 %copy.31 = bf16[2,768,256]{2,1,0:T(8,128)(2,1)} copy(bf16[2,768,256]{2,1,0:T(8,128)(2,1)} %all_gather.7) | data formatting | bytes 1572864
  (1 shorter events, 0.0 us)
Async XLA Ops:
  7.2 75.5 %copy-start = (f32[2,768,256]{2,1,0:T(8,128)S(1)}, f32[2,768,256]{2,1,0:T(8,128)}, u32[]{:S(2)}) copy-start(f32[2,768,256]{2,1,0:T(8,128)} %param.7) | copy-start | bytes 4718596
  7.2 75.5 %all-reduce.3.cloned.1.call-start = ((), (), s32[]{:S(2)}) async-start(), calls=%async_computation | async-start | bytes 3145728 | tf_op jit(solution)/shard_map/psum | solution.py:36
  9.8 137.8 %all-reduce.5.cloned.1.call-start = ((), (), s32[]{:S(2)}) async-start(), calls=%async_computation.1 | async-start | bytes 3145728 | tf_op jit(solution)/shard_map/psum | solution.py:39
  82.7 4.2 %copy-start.2 = (f32[2,768,256]{2,1,0:T(8,128)S(1)}, f32[2,768,256]{2,1,0:T(8,128)}, u32[]{:S(2)}) copy-start(f32[2,768,256]{2,1,0:T(8,128)} %all-reduce.3.cloned.1.call-done) | copy-start | bytes 4718596
  89.5 0.9 copy-start.3
  89.5 1.0 copy-start.4
  147.6 1.9 %copy-start.1 = (f32[2,768,256]{1,2,0:T(8,128)S(1)}, f32[2,768,256]{1,2,0:T(8,128)}, u32[]{:S(2)}) copy-start(f32[2,768,256]{1,2,0:T(8,128)} %all-reduce.5.cloned.1.call-done) | copy-start | bytes 4718596
Sparse Core Ops, SparseCore 0:
  10.9 71.6 all-reduce.2
  89.7 57.8 all-reduce.4
where the time goes:
time: 174 us
  waiting for transfers between devices  93.7 us (54%)
  blocking collectives  34 us (20%)
  matrix products  22.3 us (13%)
  between operations  14.1 us (8%)
  other arithmetic  5.1 us (3%)
  local copies, waits for them, and re-layouts  4.67 us (3%)
    psum x1, waiting for transfers between devices, shards(): totals = lax.psum(local_grad, 'dp')  72.8 us
    psum x1, waiting for transfers between devices, shards(): subspace = lax.psum(partial_sub, 'mp')  20.9 us
    all_gather x1, blocking collectives, shards(): new_weights = lax.all_gather(updated, 'dp', axis=1, tiled=True)  18.3 us
    all_gather x1, blocking collectives, back_project(): lax.all_gather(direction_own, 'dp', axis=1, tiled=True)  15.7 us
    dot_general x4, matrix products, newton_schulz(): jnp.einsum('ldr,lrs->lds', current, gram, precision=highest)  7.29 us
    dot_general x4, matrix products, newton_schulz(): gram = jnp.einsum('ldr,lds->lrs', current, current, precision=highest)  6.66 us
    unnamed x12, local copies, waits for them, and re-layouts  4.67 us
    dot_general x1, matrix products, shards(): lowrank = jnp.einsum('ldr,ldf->lrf', projection, totals, precision=highest)  4.21 us
  transfers between devices with their start and end apart: 2, of which 2 were waited for; matrix products, arithmetic and copies ran while one was open for 1% of the time, Pallas kernels for 0%

commit v1 on v0

--- a/solution.py
+++ b/solution.py
@@ -36,7 +36,7 @@
     totals = lax.psum(local_grad, "dp")
     lowrank = jnp.einsum("ldr,ldf->lrf", projection, totals, precision=highest)
     partial_sub = jnp.einsum("ldf,lrf->ldr", totals, lowrank, precision=highest)
-    subspace = lax.psum(partial_sub, "mp")
+    subspace = jnp.sum(lax.all_gather(partial_sub, "mp"), axis=0)
     rank_rows = moment_first.shape[1]
     rank_start = lax.axis_index("dp") * rank_rows
     low_own = lax.dynamic_slice_in_dim(lowrank, rank_start, rank_rows, 1)

time: 174 us -> 199 us (1.14)
  waiting for transfers between devices: 93.7 us -> 106 us
  other arithmetic: 5.1 us -> 11.5 us
  matrix products: 22.3 us -> 26.6 us
    all_gather x0 -> x1, waiting for transfers between devices: none -> 33.2 us  [shards(): subspace = jnp.sum(lax.all_gather(partial_sub, 'mp'), axis=0)]
    psum x1 -> x0, waiting for transfers between devices: 20.9 us -> none  [shards(): subspace = lax.psum(partial_sub, 'mp')]
    reduce_sum x0 -> x1, other arithmetic: none -> 5.6 us  [shards(): subspace = jnp.sum(lax.all_gather(partial_sub, 'mp'), axis=0)]
    dot_general x4, matrix products: 6.66 us -> 11.5 us  [newton_schulz(): gram = jnp.einsum('ldr,lds->lrs', current, current, precision=highest)]
    unnamed x12 -> x14, local copies, waits for them, and re-layouts: 4.67 us -> 4.23 us
  transfers between devices with their start and end apart: 2 -> 2, of which waited for: 2 -> 2; matrix products, arithmetic and copies ran while one was open for 1% -> 2% of each run, Pallas kernels for 0% -> 0%
where the time goes in v1:
time: 199 us; the launch traced here: 198 us
  waiting for transfers between devices  106 us (53%)
  blocking collectives  34 us (17%)
  matrix products  26.6 us (13%)
  between operations  14.2 us (7%)
  other arithmetic  11.5 us (6%)
  local copies, waits for them, and re-layouts  5.85 us (3%)
    psum x1, waiting for transfers between devices, shards(): totals = lax.psum(local_grad, 'dp')  72.8 us
    all_gather x1, waiting for transfers between devices, shards(): subspace = jnp.sum(lax.all_gather(partial_sub, 'mp'), axis=0)  33.2 us
    all_gather x1, blocking collectives, shards(): new_weights = lax.all_gather(updated, 'dp', axis=1, tiled=True)  18.3 us
    all_gather x1, blocking collectives, back_project(): lax.all_gather(direction_own, 'dp', axis=1, tiled=True)  15.7 us
    dot_general x4, matrix products, newton_schulz(): gram = jnp.einsum('ldr,lds->lrs', current, current, precision=highest)  11.5 us
    dot_general x4, matrix products, newton_schulz(): jnp.einsum('ldr,lrs->lds', current, gram, precision=highest)  7.9 us
    reduce_sum x1, other arithmetic, shards(): subspace = jnp.sum(lax.all_gather(partial_sub, 'mp'), axis=0)  5.6 us
    unnamed x14, local copies, waits for them, and re-layouts  4.23 us
  transfers between devices with their start and end apart: 2, of which 2 were waited for; matrix products, arithmetic and copies ran while one was open for 2% of the time, Pallas kernels for 0%

profile of v1, /device:TPU:0, one launch (start us, length us, event | category | flops | bytes accessed | tf_op | source)
XLA Modules:
  0.0 198.2 jit_solution(3828468764391465688)
XLA Ops:
  7.2 0.0 copy-start
  7.2 0.0 all-reduce.2.cloned.1.call-start
  7.2 2.5 %bitcast_convert_fusion = f32[2,768,256]{2,1,0:T(8,128)} fusion(bf16[1,2,768,256]{3,2,1,0:T(8,128)(2,1)} %param.5), kind=kLoop, calls=%fused_computation.12 | loop fusion | flops 393216 | bytes 2359296 | tf_op jit(solution)/shard_map/convert_element_type | solution.py:35
  9.7 0.0 all-reduce.2.cloned.1.call-update
  9.8 0.0 all-gather.3.cloned.1.call-start
  9.8 72.8 %all-reduce.2.cloned.1.call-done = f32[2,768,256]{2,1,0:T(8,128)} async-done(((f32[2,768,256]{2,1,0:T(8,128)}), f32[2,768,256]{2,1,0:T(8,128)}) %all-reduce.2.cloned.1.call-update) | async-done | bytes 1572880 | tf_op jit(solution)/shard_map/psum | solution.py:36
  82.7 0.0 copy-done
  82.7 0.0 copy-start.1
  82.7 4.2 %fusion.11 = f32[2,256,256]{2,1,0:T(8,128)S(1)} fusion(f32[2,768,256]{2,1,0:T(8,128)S(1)} %copy-done, f32[2,768,256]{2,1,0:T(8,128)} %all-reduce.2.cloned.1.call-done), kind=kOutput, calls=%fused_computation.22 | convolution fusion | flops 1207959552 | bytes 3670016 | tf_op jit(solution)/shard_map/ldr,ldf->lrf/dot_general | solution.py:37
  86.9 0.0 copy-start.3
  86.9 0.8 copy-done.3
  87.7 0.0 copy-done.1
  87.7 1.5 convolution_bitcast_fusion
  89.2 1.6 copy.11
  90.8 0.0 copy-start.4
  90.8 0.0 copy-start.5
  90.8 0.0 all-gather.3.cloned.1.call-update
  90.8 0.9 copy-done.4
  91.7 0.1 copy-done.5
  91.7 1.7 add_divide_fusion
  93.4 15.7 %all_gather.12 = f32[2,256,256]{2,1,0:T(8,128)S(1)} all-gather(f32[2,64,256]{2,1,0:T(8,128)S(1)} %get-tuple-element.4), channel_id=1, replica_groups=mesh['dp'=4,'mp'=8] {'dp'}, dimensions={1}, use_global_device_ids=true | all-gather | bytes 655360 | tf_op jit(solution)/shard_map/all_gather | solution.py:28
  109.1 1.5 fusion.4
  110.6 18.3 %all_gather.13 = bf16[2,768,256]{2,1,0:T(8,128)(2,1)} all-gather(bf16[2,192,256]{2,1,0:T(8,128)(2,1)S(1)} %fusion.4), channel_id=1, replica_groups=mesh['dp'=4,'mp'=8] {'dp'}, dimensions={1}, use_global_device_ids=true | all-gather | bytes 983040 | tf_op jit(solution)/shard_map/all_gather | solution.py:52
  128.9 33.2 %all-gather.3.cloned.1.call-done = f32[16,768,256]{2,1,0:T(8,128)} async-done(((f32[2,768,256]{2,1,0:T(8,128)}), f32[16,768,256]{2,1,0:T(8,128)}) %all-gather.3.cloned.1.call-update) | async-done | bytes 12582928 | tf_op jit(solution)/shard_map/all_gather | solution.py:39
  162.1 5.6 %reduce_sum.18 = f32[2,768,256]{2,1,0:T(8,128)S(1)} reduce(f32[8,2,768,256]{3,2,1,0:T(8,128)} %bitcast.24, f32[]{:T(128)} %constant.8.clone.1), dimensions={0}, to_apply=%region_1.0 | reduce | flops 2752512 | bytes 14155780 | tf_op jit(solution)/shard_map/reduce_sum | solution.py:39
  167.7 1.6 copy.15
  169.3 1.7 multiply_reduce_fusion
  171.1 2.8 %fusion = f32[2,256,256]{2,1,0:T(8,128)S(1)} fusion(f32[2,768,256]{2,1,0:T(8,128)S(1)} %reduce_sum.18, f32[2]{0:T(128)S(1)} %add_divide_fusion.1), kind=kOutput, calls=%fused_computation.6 | convolution fusion | flops 1208352768 | bytes 2097160 | tf_op jit(solution)/shard_map/ldr,lds->lrs/dot_general | solution.py:18
  173.9 1.8 multiply_subtract_fusion.3
  175.7 2.8 %fusion.12 = f32[2,256,256]{2,1,0:T(8,128)S(1)} fusion(f32[2,768,256]{2,1,0:T(8,128)S(1)} %multiply_subtract_fusion.3), kind=kOutput, calls=%fused_computation.23 | convolution fusion | flops 1207959552 | bytes 2097152 | tf_op jit(solution)/shard_map/ldr,lds->lrs/dot_general | solution.py:18
  178.5 1.7 multiply_subtract_fusion.2
  180.2 3.0 %fusion.13 = f32[2,256,256]{2,1,0:T(8,128)S(1)} fusion(f32[2,768,256]{2,1,0:T(8,128)S(1)} %multiply_subtract_fusion.2), kind=kOutput, calls=%fused_computation.24 | convolution fusion | flops 1207959552 | bytes 2097152 | tf_op jit(solution)/shard_map/ldr,lds->lrs/dot_general | solution.py:18
  183.2 1.7 multiply_subtract_fusion.1
  184.9 2.8 %fusion.14 = f32[2,256,256]{2,1,0:T(8,128)S(1)} fusion(f32[2,768,256]{2,1,0:T(8,128)S(1)} %multiply_subtract_fusion.1), kind=kOutput, calls=%fused_computation.25 | convolution fusion | flops 1207959552 | bytes 2097152 | tf_op jit(solution)/shard_map/ldr,lds->lrs/dot_general | solution.py:18
  187.7 0.0 copy-start.2
  187.7 2.8 %multiply_subtract_fusion = f32[2,768,256]{2,1,0:T(8,128)} fusion(f32[2,768,256]{2,1,0:T(8,128)S(1)} %multiply_subtract_fusion.1, f32[2,256,256]{2,1,0:T(8,128)S(1)} %fusion.14), kind=kOutput, calls=%fused_computation | convolution fusion | flops 1209139200 | bytes 3670016 | tf_op jit(solution)/shard_map/ldr,lrs->lds/dot_general | solution.py:19
  190.5 0.0 copy-done.2
  190.5 0.9 copy.18
  (1 shorter events, 0.0 us)
Async XLA Ops:
  7.2 75.5 %copy-start = (f32[2,768,256]{2,1,0:T(8,128)S(1)}, f32[2,768,256]{2,1,0:T(8,128)}, u32[]{:S(2)}) copy-start(f32[2,768,256]{2,1,0:T(8,128)} %param.7) | copy-start | bytes 4718596
  7.2 75.5 %all-reduce.2.cloned.1.call-start = ((), (), s32[]{:S(2)}) async-start(), calls=%async_computation | async-start | bytes 3145728 | tf_op jit(solution)/shard_map/psum | solution.py:36
  9.8 152.4 %all-gather.3.cloned.1.call-start = ((), (), s32[]{:S(2)}) async-start(), calls=%async_computation.1 | async-start | bytes 14155776 | tf_op jit(solution)/shard_map/all_gather | solution.py:39
  82.7 5.0 %copy-start.1 = (f32[2,768,256]{2,1,0:T(8,128)S(1)}, f32[2,768,256]{2,1,0:T(8,128)}, u32[]{:S(2)}) copy-start(f32[2,768,256]{2,1,0:T(8,128)} %all-reduce.2.cloned.1.call-done) | copy-start | bytes 4718596
  86.9 0.8 copy-start.3
  90.8 0.9 copy-start.4
  90.8 1.0 copy-start.5
  187.7 2.8 %copy-start.2 = (bf16[2,768,256]{2,1,0:T(8,128)(2,1)S(1)}, bf16[2,768,256]{2,1,0:T(8,128)(2,1)}, u32[]{:S(2)}) copy-start(bf16[2,768,256]{2,1,0:T(8,128)(2,1)} %all_gather.13) | copy-start | bytes 2359300
Sparse Core Ops, SparseCore 0:
  10.9 71.6 all-reduce.1
  90.9 71.1 all-gather.2
